TPU v7x, 32 devices: a whole 2x2x4 slice. The times are simulated.
32 devices in a mesh: dp: 16 (over z, y, core), tensor: 2 (over x).
Axes of the slice: x: 2, y: 2, z: 4, core: 2. Of those that a mesh axis runs over, the one named last changes fastest.
Arguments:
- tokens: bfloat16 [32, 448, 1024], P('dp'), may hold values from -6 to 6
- encoded: bfloat16 [32, 1500, 1024], P('dp'), may hold values from -6 to 6
- cotangent: bfloat16 [32, 448, 1024], P('dp'), may hold values from -6 to 6
- self_gain: bfloat16 [1024], replicated, may hold values from 0.5 to 1.5
- self_shift: bfloat16 [1024], replicated, may hold values from -1.75 to 1.75
- self_query: bfloat16 [1024, 1024], P(None, 'tensor'), may hold values from -0.25 to 0.25
- self_query_bias: bfloat16 [1024], P('tensor'), may hold values from -1.75 to 1.75
- self_key: bfloat16 [1024, 1024], P(None, 'tensor'), may hold values from -0.1875 to 0.1875
- self_value: bfloat16 [1024, 1024], P(None, 'tensor'), may hold values from -0.1875 to 0.1875
- self_value_bias: bfloat16 [1024], P('tensor'), may hold values from -1.75 to 1.75
- self_mixer: bfloat16 [1024, 1024], P('tensor'), may hold values from -0.5 to 0.5
- self_mixer_bias: bfloat16 [1024], replicated, may hold values from -1.75 to 1.75
- cross_gain: bfloat16 [1024], replicated, may hold values from 0.5 to 1.5
- cross_shift: bfloat16 [1024], replicated, may hold values from -1.75 to 1.75
- cross_query: bfloat16 [1024, 1024], P(None, 'tensor'), may hold values from -0.25 to 0.25
- cross_query_bias: bfloat16 [1024], P('tensor'), may hold values from -1.75 to 1.75
- cross_key: bfloat16 [1024, 1024], P(None, 'tensor'), may hold values from -0.1875 to 0.1875
- cross_value: bfloat16 [1024, 1024], P(None, 'tensor'), may hold values from -0.1875 to 0.1875
- cross_value_bias: bfloat16 [1024], P('tensor'), may hold values from -1.75 to 1.75
- cross_mixer: bfloat16 [1024, 1024], P('tensor'), may hold values from -0.75 to 0.75
- cross_mixer_bias: bfloat16 [1024], replicated, may hold values from -1.75 to 1.75
- feed_gain: bfloat16 [1024], replicated, may hold values from 0.5 to 1.5
- feed_shift: bfloat16 [1024], replicated, may hold values from -1.75 to 1.75
- expand_weight: bfloat16 [1024, 4096], P(None, 'tensor'), may hold values from -0.1875 to 0.1875
- expand_bias: bfloat16 [4096], P('tensor'), may hold values from -3 to 3
- reduce_weight: bfloat16 [4096, 1024], P('tensor'), may hold values from -0.125 to 0.125
- reduce_bias: bfloat16 [1024], replicated, may hold values from -1.75 to 1.75
Outputs:
- output: float32 [32, 448, 1024], P('dp')
- grad_tokens: float32 [32, 448, 1024], P('dp')
- grad_encoded: float32 [32, 1500, 1024], P('dp', None, 'tensor')
- grad_self_gain: float32 [1024], replicated
- grad_self_shift: float32 [1024], replicated
- grad_self_query: float32 [1024, 1024], P(None, 'tensor')
- grad_self_query_bias: float32 [1024], P('tensor')
- grad_self_key: float32 [1024, 1024], P(None, 'tensor')
- grad_self_value: float32 [1024, 1024], P(None, 'tensor')
- grad_self_value_bias: float32 [1024], P('tensor')
- grad_self_mixer: float32 [1024, 1024], P('tensor')
- grad_self_mixer_bias: float32 [1024], replicated
- grad_cross_gain: float32 [1024], replicated
- grad_cross_shift: float32 [1024], replicated
- grad_cross_query: float32 [1024, 1024], P(None, 'tensor')
- grad_cross_query_bias: float32 [1024], P('tensor')
- grad_cross_key: float32 [1024, 1024], P(None, 'tensor')
- grad_cross_value: float32 [1024, 1024], P(None, 'tensor')
- grad_cross_value_bias: float32 [1024], P('tensor')
- grad_cross_mixer: float32 [1024, 1024], P('tensor')
- grad_cross_mixer_bias: float32 [1024], replicated
- grad_feed_gain: float32 [1024], replicated
- grad_feed_shift: float32 [1024], replicated
- grad_expand_weight: float32 [1024, 4096], P(None, 'tensor')
- grad_expand_bias: float32 [4096], P('tensor')
- grad_reduce_weight: float32 [4096, 1024], P('tensor')
- grad_reduce_bias: float32 [1024], replicated
All inputs are finite; a program needn't handle non-finite values.
Results may differ from a plain program's by a relative error of at most 0.022.
Values may be sent and summed in bfloat16 or wider, within the bound.
No kernel may reach another device: no remote copies, remote signals or barrier semaphores. Data moves between devices by JAX's collectives and lax.ppermute only.
A program may use at most 256 MiB of HBM per device.

v0:
```python
import math
import jax
import jax.numpy as jnp
from jax import lax
from jax.sharding import PartitionSpec as P

HEAD = 64
EPSILON = 1e-05
F32 = jnp.float32
BF16 = jnp.bfloat16


def normalize(values, norm_gain, norm_shift):
    row_mean = jnp.mean(values, axis=-1, keepdims=True)
    centered = values - row_mean
    spread = jnp.mean(centered * centered, axis=-1, keepdims=True)
    inverse = lax.rsqrt(spread + EPSILON)
    normed = centered * inverse
    return (normed * norm_gain + norm_shift, normed, inverse)


def normalize_back(grad_out, normed, inverse, norm_gain):
    scaled = grad_out * norm_gain
    centre = jnp.mean(scaled, axis=-1, keepdims=True)
    row_along = jnp.mean(scaled * normed, axis=-1, keepdims=True)
    grad_in = inverse * (scaled - centre - normed * row_along)
    return (grad_in, jnp.sum(grad_out * normed, axis=0), jnp.sum(grad_out, axis=0))


def scores_of(queries, key_heads, causal):
    scaling = 1.0 / math.sqrt(queries.shape[-1])
    scores = jnp.einsum("lhe,khe->hlk", queries, key_heads, preferred_element_type=F32) * scaling
    if causal:
        row_index = lax.broadcasted_iota(jnp.int32, scores.shape[-2:], 0)
        col_index = lax.broadcasted_iota(jnp.int32, scores.shape[-2:], 1)
        scores = jnp.where(col_index <= row_index, scores, -1e30)
    return scores


def attend(queries, key_heads, value_heads, causal):
    scores = scores_of(queries, key_heads, causal)
    highest = jnp.max(scores, axis=-1, keepdims=True)
    denominator = jnp.sum(jnp.exp(scores - highest), axis=-1, keepdims=True)
    logsum = highest + jnp.log(denominator)
    probs = jnp.exp(scores - logsum)
    mixture = jnp.einsum(
        "hlk,khe->lhe", probs.astype(BF16), value_heads, preferred_element_type=F32
    )
    return (mixture.astype(BF16), logsum)


def attend_back(grad_mixture, queries, key_heads, value_heads, logsum, causal):
    scaling = 1.0 / math.sqrt(queries.shape[-1])
    probs = jnp.exp(scores_of(queries, key_heads, causal) - logsum)
    grad_probs = jnp.einsum("lhe,khe->hlk", grad_mixture, value_heads, preferred_element_type=F32)
    row_dot = jnp.sum(grad_probs * probs, axis=-1, keepdims=True)
    grad_scores = (probs * (grad_probs - row_dot)).astype(BF16)
    grad_queries = (
        jnp.einsum("hlk,khe->lhe", grad_scores, key_heads, preferred_element_type=F32) * scaling
    ).astype(BF16)
    grad_keys = (
        jnp.einsum("hlk,lhe->khe", grad_scores, queries, preferred_element_type=F32) * scaling
    ).astype(BF16)
    grad_values = jnp.einsum(
        "hlk,lhe->khe", probs.astype(BF16), grad_mixture, preferred_element_type=F32
    ).astype(BF16)
    return (grad_queries, grad_keys, grad_values)


def project(inputs, weight):
    return jnp.dot(inputs, weight, preferred_element_type=F32)


def project_back(grads, weight):
    return jnp.einsum("lc,dc->ld", grads, weight, preferred_element_type=F32)


def weight_grad(inputs, grads):
    left = jnp.concatenate(inputs, axis=0)
    right = jnp.concatenate(grads, axis=0)
    return jnp.einsum("ld,lc->dc", left, right, preferred_element_type=F32).astype(BF16)


def column_sum(grads):
    return jnp.sum(grads.astype(F32), axis=0)


def tensor_sum(partial):
    if lax.axis_size("tensor") != 2:
        return lax.psum(partial, "tensor")
    mine = lax.optimization_barrier(partial.astype(BF16))
    other = lax.ppermute(mine, "tensor", [(0, 1), (1, 0)])
    return mine.astype(F32) + other.astype(F32)


def dp_sum(grads):
    share = lax.psum_scatter(grads, "dp", scatter_dimension=0, tiled=True)
    return lax.all_gather(share, "dp", axis=0, tiled=True)


def local(
    tokens,
    encoded,
    cotangent,
    self_gain,
    self_shift,
    self_query,
    self_query_bias,
    self_key,
    self_value,
    self_value_bias,
    self_mixer,
    self_mixer_bias,
    cross_gain,
    cross_shift,
    cross_query,
    cross_query_bias,
    cross_key,
    cross_value,
    cross_value_bias,
    cross_mixer,
    cross_mixer_bias,
    feed_gain,
    feed_shift,
    expand_weight,
    expand_bias,
    reduce_weight,
    reduce_bias,
):
    clips, length, width = tokens.shape
    frames = encoded.shape[1]
    local_width = self_query.shape[1]
    head_count = local_width // HEAD
    gain_one = self_gain.astype(F32)
    gain_two = cross_gain.astype(F32)
    gain_three = feed_gain.astype(F32)
    each = range(clips)

    def heads(values):
        return values.reshape(values.shape[0], head_count, HEAD)

    def flat(values):
        return values.reshape(values.shape[0], local_width)

    source, normed_one, inverse_one, attn_in = ([], [], [], [])
    self_queries, self_keys, self_values = ([], [], [])
    self_mixture, self_logsum, self_sum = ([], [], [])
    cross_keys, cross_values = ([], [])
    for i in each:
        source.append(tokens[i].astype(F32))
        normed, plain, inverse = normalize(source[i], gain_one, self_shift.astype(F32))
        normed_one.append(plain)
        inverse_one.append(inverse)
        attn_in.append(normed.astype(BF16))
        self_queries.append(
            (project(attn_in[i], self_query) + self_query_bias.astype(F32)).astype(BF16)
        )
        self_keys.append(project(attn_in[i], self_key).astype(BF16))
        self_values.append(
            (project(attn_in[i], self_value) + self_value_bias.astype(F32)).astype(BF16)
        )
        mixed, logsum = attend(
            heads(self_queries[i]), heads(self_keys[i]), heads(self_values[i]), True
        )
        self_mixture.append(flat(mixed))
        self_logsum.append(logsum)
        self_sum.append(tensor_sum(project(self_mixture[i], self_mixer)))
    for i in each:
        cross_keys.append(project(encoded[i], cross_key).astype(BF16))
        cross_values.append(
            (project(encoded[i], cross_value) + cross_value_bias.astype(F32)).astype(BF16)
        )
    hidden_one, normed_two, inverse_two, cross_in = ([], [], [], [])
    cross_queries, cross_mixture, cross_logsum, cross_sum = ([], [], [], [])
    for i in each:
        hidden_one.append(source[i] + self_sum[i] + self_mixer_bias.astype(F32))
        normed, plain, inverse = normalize(hidden_one[i], gain_two, cross_shift.astype(F32))
        normed_two.append(plain)
        inverse_two.append(inverse)
        cross_in.append(normed.astype(BF16))
        cross_queries.append(
            (project(cross_in[i], cross_query) + cross_query_bias.astype(F32)).astype(BF16)
        )
        mixed, logsum = attend(
            heads(cross_queries[i]), heads(cross_keys[i]), heads(cross_values[i]), False
        )
        cross_mixture.append(flat(mixed))
        cross_logsum.append(logsum)
        cross_sum.append(tensor_sum(project(cross_mixture[i], cross_mixer)))
    hidden_two, normed_three, inverse_three, feed_in = ([], [], [], [])
    activated, grad_preact, feed_grad, feed_sum = ([], [], [], [])
    for i in each:
        hidden_two.append(hidden_one[i] + cross_sum[i] + cross_mixer_bias.astype(F32))
        normed, plain, inverse = normalize(hidden_two[i], gain_three, feed_shift.astype(F32))
        normed_three.append(plain)
        inverse_three.append(inverse)
        feed_in.append(normed.astype(BF16))
        preact = project(feed_in[i], expand_weight) + expand_bias.astype(F32)
        grad_activated = project_back(cotangent[i], reduce_weight)
        cdf = 0.5 * (1.0 + lax.erf(preact * (1.0 / math.sqrt(2.0))))
        density = jnp.exp(-0.5 * preact * preact) * (1.0 / math.sqrt(2.0 * math.pi))
        activated.append((preact * cdf).astype(BF16))
        grad_preact.append((grad_activated * (cdf + preact * density)).astype(BF16))
        feed_grad.append(tensor_sum(project_back(grad_preact[i], expand_weight)))
    for i in each:
        feed_sum.append(tensor_sum(project(activated[i], reduce_weight)))
    output = [hidden_two[i] + feed_sum[i] + reduce_bias.astype(F32) for i in each]
    grad_out = [cotangent[i].astype(F32) for i in each]
    grad_reduce_weight = dp_sum(weight_grad(activated, [cotangent[i] for i in each]))
    grad_expand_weight = dp_sum(weight_grad(feed_in, grad_preact))
    grad_reduce_bias = sum((jnp.sum(grad_out[i], axis=0) for i in each))
    grad_expand_bias = sum((column_sum(grad_preact[i]) for i in each))
    grad_two, two_rounded, feed_gains, feed_shifts = ([], [], [], [])
    cross_query_grad, cross_key_grad, cross_value_grad = ([], [], [])
    cross_grad = []
    for i in each:
        norm_grad, part_gain, part_shift = normalize_back(
            feed_grad[i], normed_three[i], inverse_three[i], gain_three
        )
        feed_gains.append(part_gain)
        feed_shifts.append(part_shift)
        grad_two.append(grad_out[i] + norm_grad)
        two_rounded.append(grad_two[i].astype(BF16))
        grad_cross_mixture = project_back(two_rounded[i], cross_mixer).astype(BF16)
        query_grad, key_grad, value_grad = attend_back(
            heads(grad_cross_mixture),
            heads(cross_queries[i]),
            heads(cross_keys[i]),
            heads(cross_values[i]),
            cross_logsum[i],
            False,
        )
        cross_query_grad.append(flat(query_grad))
        cross_key_grad.append(flat(key_grad))
        cross_value_grad.append(flat(value_grad))
        cross_grad.append(tensor_sum(project_back(cross_query_grad[i], cross_query)))
    grad_cross_mixer = dp_sum(weight_grad(cross_mixture, two_rounded))
    grad_cross_query = dp_sum(weight_grad(cross_in, cross_query_grad))
    frames_in = [encoded[i] for i in each]
    grad_cross_key = dp_sum(weight_grad(frames_in, cross_key_grad))
    grad_cross_value = dp_sum(weight_grad(frames_in, cross_value_grad))
    part_cross_mixer_bias = sum((jnp.sum(grad_two[i], axis=0) for i in each))
    grad_cross_query_bias = sum((column_sum(cross_query_grad[i]) for i in each))
    grad_cross_value_bias = sum((column_sum(cross_value_grad[i]) for i in each))
    grad_one, one_rounded, cross_gains, cross_shifts = ([], [], [], [])
    query_grads, key_grads, value_grads, self_grad = ([], [], [], [])
    for i in each:
        norm_grad, part_gain, part_shift = normalize_back(
            cross_grad[i], normed_two[i], inverse_two[i], gain_two
        )
        cross_gains.append(part_gain)
        cross_shifts.append(part_shift)
        grad_one.append(grad_two[i] + norm_grad)
        one_rounded.append(grad_one[i].astype(BF16))
        grad_self_mixture = project_back(one_rounded[i], self_mixer).astype(BF16)
        query_grad, key_grad, value_grad = attend_back(
            heads(grad_self_mixture),
            heads(self_queries[i]),
            heads(self_keys[i]),
            heads(self_values[i]),
            self_logsum[i],
            True,
        )
        query_grads.append(flat(query_grad))
        key_grads.append(flat(key_grad))
        value_grads.append(flat(value_grad))
        self_terms = (
            project_back(query_grads[i], self_query)
            + project_back(key_grads[i], self_key)
            + project_back(value_grads[i], self_value)
        )
        self_grad.append(tensor_sum(self_terms))
    grad_self_mixer = dp_sum(weight_grad(self_mixture, one_rounded))
    grad_self_query = dp_sum(weight_grad(attn_in, query_grads))
    grad_self_key = dp_sum(weight_grad(attn_in, key_grads))
    grad_self_value = dp_sum(weight_grad(attn_in, value_grads))
    part_self_mixer_bias = sum((jnp.sum(grad_one[i], axis=0) for i in each))
    grad_self_query_bias = sum((column_sum(query_grads[i]) for i in each))
    grad_self_value_bias = sum((column_sum(value_grads[i]) for i in each))
    grad_encoded = []
    members = lax.axis_size("tensor")
    share = width // members
    for i in each:
        if members == 2:
            me = lax.axis_index("tensor")

            def terms(part):
                rows_key = lax.dynamic_slice_in_dim(cross_key, part * share, share, 0)
                rows_value = lax.dynamic_slice_in_dim(cross_value, part * share, share, 0)
                return project_back(cross_key_grad[i], rows_key) + project_back(
                    cross_value_grad[i], rows_value
                )

            other = lax.ppermute(terms(1 - me).astype(BF16), "tensor", [(0, 1), (1, 0)])
            grad_encoded.append(terms(me) + other.astype(F32))
        else:
            frame_terms = project_back(cross_key_grad[i], cross_key) + project_back(
                cross_value_grad[i], cross_value
            )
            grad_encoded.append(
                lax.psum_scatter(frame_terms, "tensor", scatter_dimension=1, tiled=True)
            )
    self_gains, self_shifts, grad_tokens = ([], [], [])
    for i in each:
        norm_grad, part_gain, part_shift = normalize_back(
            self_grad[i], normed_one[i], inverse_one[i], gain_one
        )
        self_gains.append(part_gain)
        self_shifts.append(part_shift)
        grad_tokens.append(grad_one[i] + norm_grad)
    vectors = [
        sum(self_gains),
        sum(self_shifts),
        part_self_mixer_bias,
        sum(cross_gains),
        sum(cross_shifts),
        part_cross_mixer_bias,
        sum(feed_gains),
        sum(feed_shifts),
        grad_reduce_bias,
        grad_self_query_bias,
        grad_self_value_bias,
        grad_cross_query_bias,
        grad_cross_value_bias,
        grad_expand_bias,
    ]
    summed = lax.psum(jnp.concatenate(vectors), "dp")
    pieces, offset = ([], 0)
    for piece in vectors:
        pieces.append(summed[offset : offset + piece.size])
        offset = offset + piece.size
    return (
        jnp.stack(output),
        jnp.stack(grad_tokens),
        jnp.stack(grad_encoded),
        pieces[0],
        pieces[1],
        grad_self_query.astype(F32),
        pieces[9],
        grad_self_key.astype(F32),
        grad_self_value.astype(F32),
        pieces[10],
        grad_self_mixer.astype(F32),
        pieces[2],
        pieces[3],
        pieces[4],
        grad_cross_query.astype(F32),
        pieces[11],
        grad_cross_key.astype(F32),
        grad_cross_value.astype(F32),
        pieces[12],
        grad_cross_mixer.astype(F32),
        pieces[5],
        pieces[6],
        pieces[7],
        grad_expand_weight.astype(F32),
        pieces[13],
        grad_reduce_weight.astype(F32),
        pieces[8],
    )


def solution(mesh):
    rows = P("dp", None, None)
    column, row, part = (P(None, "tensor"), P("tensor", None), P("tensor"))
    return jax.shard_map(
        local,
        mesh=mesh,
        in_specs=(
            rows,
            rows,
            rows,
            P(),
            P(),
            column,
            part,
            column,
            column,
            part,
            row,
            P(),
            P(),
            P(),
            column,
            part,
            column,
            column,
            part,
            row,
            P(),
            P(),
            P(),
            column,
            part,
            row,
            P(),
        ),
        out_specs=(
            rows,
            rows,
            P("dp", None, "tensor"),
            P(),
            P(),
            column,
            part,
            column,
            column,
            part,
            row,
            P(),
            P(),
            P(),
            column,
            part,
            column,
            column,
            part,
            row,
            P(),
            P(),
            P(),
            column,
            part,
            row,
            P(),
        ),
        check_vma=False,
    )
```

profile of v0, /device:TPU:0, one launch (start us, length us, event | category | flops | bytes accessed | tf_op | source)
XLA Modules:
  0.0 1475.0 jit_solution(17825031323830864179)
XLA Ops:
  41.3 9.7 fusion.219
  51.0 8.1 copy_bitcast_fusion
  86.2 5.9 exponential_reduce_fusion.1
  93.5 12.3 fusion.135
  108.2 21.7 %collective-permute-done.1 = bf16[448,1024]{1,0:T(8,128)(2,1)S(1)} collective-permute-done((bf16[448,1024]{1,0:T(8,128)(2,1)S(1)}, bf16[448,1024]{1,0:T(8,128)(2,1)S(1)}, u32[]{:S(2)}, u32[]{:S(2)}) %collective-permute-start.1) | collective-permute-done | bytes 917536 | tf_op jit(solution)/shard_map/ppermute | solution.py:92
  151.8 15.1 %collective-permute-done.6 = bf16[448,1024]{1,0:T(8,128)(2,1)} collective-permute-done((bf16[448,1024]{1,0:T(8,128)(2,1)}, bf16[448,1024]{1,0:T(8,128)(2,1)}, u32[]{:S(2)}, u32[]{:S(2)}) %collective-permute-start.6) | collective-permute-done | bytes 917536 | tf_op jit(solution)/shard_map/ppermute | solution.py:92
  170.5 13.8 collective-permute-done.2
  194.5 15.2 %multiply_reduce_fusion.1 = (f32[8,448]{1,0:T(8,128)S(1)}, f32[8,448,1500]{2,1,0:T(8,128)}) fusion(f32[8,448,1500]{2,1,0:T(8,128)} %copy-done.1, f32[8,448]{1,0:T(8,128)S(1)} %log_add_fusion.2, bf16[448,8,64]{0,2,1:T(8,128)(2,1)} %bitcast.336, bf16[1500,8,64]{0,2,1:T(8,128)(2,1)} %bitcast.325), kind=kOutput, calls=%fused_computation.3 | convolution fusion | flops 709628416 | bytes 45031424 | tf_op jit(solution)/shard_map/lhe,khe->hlk/dot_general | solution.py:55
  209.7 15.0 %multiply_convert_fusion.1 = bf16[8,448,1500]{2,1,0:T(8,128)(2,1)S(1)} fusion(f32[8,448,1500]{2,1,0:T(8,128)} %get-tuple-element.165, f32[8,448,1500]{2,1,0:T(8,128)} %copy-done.1, f32[8,448]{1,0:T(8,128)S(1)} %get-tuple-element.164, f32[8,448]{1,0:T(8,128)S(1)} %log_add_fusion.2), kind=kLoop, calls=%fused_computation.2 | loop fusion | flops 26880000 | bytes 53788672 | tf_op jit(solution)/shard_map/convert_element_type | solution.py:57
  241.8 5.5 fusion.222
  247.4 5.9 collective-permute-done.7
  264.9 9.1 multiply_reduce_fusion.5
  316.1 5.7 exponential_reduce_fusion
  324.0 10.1 fusion.138
  337.3 10.9 convert_reduce_fusion.3
  348.3 6.3 collective-permute-done.4
  374.0 15.8 %collective-permute-done.9 = bf16[448,1024]{1,0:T(8,128)(2,1)S(1)} collective-permute-done((bf16[448,1024]{1,0:T(8,128)(2,1)S(1)}, bf16[448,1024]{1,0:T(8,128)(2,1)S(1)}, u32[]{:S(2)}, u32[]{:S(2)}) %collective-permute-start.9) | collective-permute-done | bytes 917536 | tf_op jit(solution)/shard_map/ppermute | solution.py:92
  391.3 12.4 collective-permute-done.5
  416.4 11.9 convert_reduce_fusion.2
  429.6 5.4 fusion.113
  435.0 15.4 %multiply_reduce_fusion = (f32[8,448]{1,0:T(8,128)S(1)}, f32[8,448,1500]{2,1,0:T(8,128)}) fusion(f32[8,448,1500]{2,1,0:T(8,128)} %copy-done.2, f32[8,448]{1,0:T(8,128)S(1)} %log_add_fusion, bf16[448,8,64]{0,2,1:T(8,128)(2,1)} %bitcast.339, bf16[1500,8,64]{0,2,1:T(8,128)(2,1)} %bitcast.322), kind=kOutput, calls=%fused_computation.1 | convolution fusion | flops 709628416 | bytes 45031424 | tf_op jit(solution)/shard_map/lhe,khe->hlk/dot_general | solution.py:55
  450.9 14.9 %multiply_convert_fusion = bf16[8,448,1500]{2,1,0:T(8,128)(2,1)S(1)} fusion(f32[8,448,1500]{2,1,0:T(8,128)} %get-tuple-element.172, f32[8,448,1500]{2,1,0:T(8,128)} %copy-done.2, f32[8,448]{1,0:T(8,128)S(1)} %get-tuple-element.171, f32[8,448]{1,0:T(8,128)S(1)} %log_add_fusion), kind=kLoop, calls=%fused_computation | loop fusion | flops 26880000 | bytes 53788672 | tf_op jit(solution)/shard_map/convert_element_type | solution.py:57
  479.2 8.1 convert_reduce_fusion.8
  490.6 5.9 convert_reduce_fusion.11
  499.3 6.6 collective-permute-done.10
  552.2 6.2 convolution_convert_fusion
  559.8 8.2 convolution_convert_fusion.1
  569.4 23.4 %reduce-scatter.21.cloned.1.call-done = bf16[64,512]{1,0:T(8,128)(2,1)} async-done(((bf16[1024,512]{1,0:T(8,128)(2,1)}), bf16[64,512]{1,0:T(8,128)(2,1)}) %reduce-scatter.21.cloned.1.call-update) | async-done | bytes 65552 | tf_op jit(solution)/shard_map/reduce_scatter | solution.py:97
  592.8 60.1 %reduce-scatter.19.cloned.1.call-done = bf16[64,512]{1,0:T(8,128)(2,1)} async-done(((bf16[1024,512]{1,0:T(8,128)(2,1)}), bf16[64,512]{1,0:T(8,128)(2,1)}) %reduce-scatter.19.cloned.1.call-update) | async-done | bytes 65552 | tf_op jit(solution)/shard_map/reduce_scatter | solution.py:97
  652.9 60.1 %reduce-scatter.15.cloned.1.call-done = bf16[64,512]{1,0:T(8,128)(2,1)} async-done(((bf16[1024,512]{1,0:T(8,128)(2,1)}), bf16[64,512]{1,0:T(8,128)(2,1)}) %reduce-scatter.15.cloned.1.call-update) | async-done | bytes 65552 | tf_op jit(solution)/shard_map/reduce_scatter | solution.py:97
  713.1 60.1 %reduce-scatter.17.cloned.1.call-done = bf16[32,1024]{1,0:T(8,128)(2,1)} async-done(((bf16[512,1024]{1,0:T(8,128)(2,1)}), bf16[32,1024]{1,0:T(8,128)(2,1)}) %reduce-scatter.17.cloned.1.call-update) | async-done | bytes 65552 | tf_op jit(solution)/shard_map/reduce_scatter | solution.py:97
  773.2 60.8 %reduce-scatter.11.cloned.1.call-done = bf16[64,512]{1,0:T(8,128)(2,1)} async-done(((bf16[1024,512]{1,0:T(8,128)(2,1)}), bf16[64,512]{1,0:T(8,128)(2,1)}) %reduce-scatter.11.cloned.1.call-update) | async-done | bytes 65552 | tf_op jit(solution)/shard_map/reduce_scatter | solution.py:97
  834.1 60.7 %reduce-scatter.13.cloned.1.call-done = bf16[64,512]{1,0:T(8,128)(2,1)} async-done(((bf16[1024,512]{1,0:T(8,128)(2,1)}), bf16[64,512]{1,0:T(8,128)(2,1)}) %reduce-scatter.13.cloned.1.call-update) | async-done | bytes 65552 | tf_op jit(solution)/shard_map/reduce_scatter | solution.py:97
  894.9 76.2 %reduce-scatter.29.cloned.1.call-done = bf16[128,1024]{1,0:T(8,128)(2,1)} async-done(((bf16[2048,1024]{1,0:T(8,128)(2,1)}), bf16[128,1024]{1,0:T(8,128)(2,1)}) %reduce-scatter.29.cloned.1.call-update) | async-done | bytes 262160 | tf_op jit(solution)/shard_map/reduce_scatter | solution.py:97
  983.4 29.0 %collective-permute-done.12 = bf16[1500,512]{1,0:T(8,128)(2,1)} collective-permute-done((bf16[1500,512]{1,0:T(8,128)(2,1)}, bf16[1500,512]{1,0:T(8,128)(2,1)}, u32[]{:S(2)}, u32[]{:S(2)}) %collective-permute-start.12) | collective-permute-done | bytes 1536032 | tf_op jit(solution)/shard_map/ppermute | solution.py:294
  1019.2 28.0 %reduce-scatter.27.cloned.1.call-done = bf16[64,2048]{1,0:T(8,128)(2,1)} async-done(((bf16[1024,2048]{1,0:T(8,128)(2,1)}), bf16[64,2048]{1,0:T(8,128)(2,1)}) %reduce-scatter.27.cloned.1.call-update) | async-done | bytes 262160 | tf_op jit(solution)/shard_map/reduce_scatter | solution.py:97
  1063.9 25.0 %collective-permute-done.13 = bf16[1500,512]{1,0:T(8,128)(2,1)} collective-permute-done((bf16[1500,512]{1,0:T(8,128)(2,1)}, bf16[1500,512]{1,0:T(8,128)(2,1)}, u32[]{:S(2)}, u32[]{:S(2)}) %collective-permute-start.13) | collective-permute-done | bytes 1536032 | tf_op jit(solution)/shard_map/ppermute | solution.py:294
  1093.7 12.7 copy.122
  1110.9 57.9 %psum.7 = f32[13312]{0:T(1024)S(1)} all-reduce(f32[13312]{0:T(1024)S(1)} %add_dynamic-update-slice_fusion), channel_id=1, replica_groups=mesh['dp'=16,'tensor'=2] {'dp'}, use_global_device_ids=true, to_apply=%region_64.65 | all-reduce | flops 13312 | bytes 106496 | tf_op jit(solution)/shard_map/psum | solution.py:327
  1185.3 17.9 %all-gather.19.cloned.1.call-done = bf16[1024,512]{1,0:T(8,128)(2,1)} async-done(((bf16[64,512]{1,0:T(8,128)(2,1)}), bf16[1024,512]{1,0:T(8,128)(2,1)}) %all-gather.19.cloned.1.call-update) | async-done | bytes 1048592 | tf_op jit(solution)/shard_map/all_gather | solution.py:98
  1206.1 36.0 %all-gather.15.cloned.1.call-done = bf16[1024,512]{1,0:T(8,128)(2,1)} async-done(((bf16[64,512]{1,0:T(8,128)(2,1)}), bf16[1024,512]{1,0:T(8,128)(2,1)}) %all-gather.15.cloned.1.call-update) | async-done | bytes 1048592 | tf_op jit(solution)/shard_map/all_gather | solution.py:98
  1245.0 36.0 %all-gather.17.cloned.1.call-done = bf16[512,1024]{1,0:T(8,128)(2,1)} async-done(((bf16[32,1024]{1,0:T(8,128)(2,1)}), bf16[512,1024]{1,0:T(8,128)(2,1)}) %all-gather.17.cloned.1.call-update) | async-done | bytes 1048592 | tf_op jit(solution)/shard_map/all_gather | solution.py:98
  1283.8 36.1 %all-gather.11.cloned.1.call-done = bf16[1024,512]{1,0:T(8,128)(2,1)} async-done(((bf16[64,512]{1,0:T(8,128)(2,1)}), bf16[1024,512]{1,0:T(8,128)(2,1)}) %all-gather.11.cloned.1.call-update) | async-done | bytes 1048592 | tf_op jit(solution)/shard_map/all_gather | solution.py:98
  1322.8 36.0 %all-gather.13.cloned.1.call-done = bf16[1024,512]{1,0:T(8,128)(2,1)} async-done(((bf16[64,512]{1,0:T(8,128)(2,1)}), bf16[1024,512]{1,0:T(8,128)(2,1)}) %all-gather.13.cloned.1.call-update) | async-done | bytes 1048592 | tf_op jit(solution)/shard_map/all_gather | solution.py:98
  1361.6 48.7 %all-gather.29.cloned.1.call-done = bf16[2048,1024]{1,0:T(8,128)(2,1)} async-done(((bf16[128,1024]{1,0:T(8,128)(2,1)}), bf16[2048,1024]{1,0:T(8,128)(2,1)}) %all-gather.29.cloned.1.call-update) | async-done | bytes 4194320 | tf_op jit(solution)/shard_map/all_gather | solution.py:98
  1410.3 6.6 convert_element_type.662
  1417.0 44.3 %all-gather.27.cloned.1.call-done = bf16[1024,2048]{1,0:T(8,128)(2,1)} async-done(((bf16[64,2048]{1,0:T(8,128)(2,1)}), bf16[1024,2048]{1,0:T(8,128)(2,1)}) %all-gather.27.cloned.1.call-update) | async-done | bytes 4194320 | tf_op jit(solution)/shard_map/all_gather | solution.py:98
  1461.3 6.7 convert_element_type.660
  (607 shorter events, 354.7 us)
Async XLA Ops:
  7.2 59.2 %copy-start = (bf16[1024,512]{1,0:T(8,128)(2,1)S(1)}, bf16[1024,512]{1,0:T(8,128)(2,1)}, u32[]{:S(2)}) copy-start(bf16[1024,512]{1,0:T(8,128)(2,1)} %param.43) | copy-start | bytes 3145732
  7.2 560.9 %reduce-scatter.25.cloned.1.call-start = ((), (), s32[]{:S(2)}) async-start(), calls=%async_computation.24 | async-start | bytes 1114112 | tf_op jit(solution)/shard_map/reduce_scatter | solution.py:97
  36.5 14.5 copy-start.155
  38.2 35.6 %collective-permute-start = (bf16[448,1024]{1,0:T(8,128)(2,1)}, bf16[448,1024]{1,0:T(8,128)(2,1)}, u32[]{:S(2)}, u32[]{:S(2)}) collective-permute-start(bf16[448,1024]{1,0:T(8,128)(2,1)} %convolution_convert_fusion.14), channel_id=1, source_target_pairs={{0,1},{1,0},{2,3},{3,2},{4,5},{5,4},{6,7},{7,6},{8,9},{9,8},{10,11... | collective-permute-start | bytes 2752520 | tf_op jit(solution)/shard_map/ppermute | solution.py:92
  105.9 24.1 %copy-start.11 = (f32[448,1024]{1,0:T(8,128)S(1)}, f32[448,1024]{1,0:T(8,128)}, u32[]{:S(2)}) copy-start(f32[448,1024]{1,0:T(8,128)} %copy-done.10) | copy-start | bytes 5505028
  108.1 21.9 %collective-permute-start.1 = (bf16[448,1024]{1,0:T(8,128)(2,1)S(1)}, bf16[448,1024]{1,0:T(8,128)(2,1)S(1)}, u32[]{:S(2)}, u32[]{:S(2)}) collective-permute-start(bf16[448,1024]{1,0:T(8,128)(2,1)S(1)} %convolution_convert_fusion.13), channel_id=1, source_target_pairs={{0,1},{1,0},{2,3},{3,2},{4,5},{5,4},{6,7},{7,6},{8,9},{9,8},{10,11... | collective-permute-start | bytes 2752520 | tf_op jit(solution)/shard_map/ppermute | solution.py:92
  143.3 23.5 %collective-permute-start.6 = (bf16[448,1024]{1,0:T(8,128)(2,1)}, bf16[448,1024]{1,0:T(8,128)(2,1)}, u32[]{:S(2)}, u32[]{:S(2)}) collective-permute-start(bf16[448,1024]{1,0:T(8,128)(2,1)} %convolution_convert_fusion.16), channel_id=1, source_target_pairs={{0,1},{1,0},{2,3},{3,2},{4,5},{5,4},{6,7},{7,6},{8,9},{9,8},{10,11... | collective-permute-start | bytes 2752520 | tf_op jit(solution)/shard_map/ppermute | solution.py:92
  146.6 37.6 %collective-permute-start.2 = (bf16[448,1024]{1,0:T(8,128)(2,1)}, bf16[448,1024]{1,0:T(8,128)(2,1)}, u32[]{:S(2)}, u32[]{:S(2)}) collective-permute-start(bf16[448,1024]{1,0:T(8,128)(2,1)} %convolution_convert_fusion.18), channel_id=1, source_target_pairs={{0,1},{1,0},{2,3},{3,2},{4,5},{5,4},{6,7},{7,6},{8,9},{9,8},{10,11... | collective-permute-start | bytes 2752520 | tf_op jit(solution)/shard_map/ppermute | solution.py:92
  151.8 32.5 %copy-start.14 = (f32[448,1024]{1,0:T(8,128)S(1)}, f32[448,1024]{1,0:T(8,128)}, u32[]{:S(2)}) copy-start(f32[448,1024]{1,0:T(8,128)} %copy-done.13) | copy-start | bytes 5505028
  151.8 32.5 %copy-start.37 = (bf16[2,448,1024]{2,1,0:T(8,128)(2,1)S(1)}, bf16[2,448,1024]{2,1,0:T(8,128)(2,1)}, u32[]{:S(2)}) copy-start(bf16[2,448,1024]{2,1,0:T(8,128)(2,1)} %param.29) | copy-start | bytes 5505028
  209.7 15.0 %copy-start.22 = (bf16[1500,512]{0,1:T(8,128)(2,1)S(1)}, bf16[1500,512]{0,1:T(8,128)(2,1)}, u32[]{:S(2)}) copy-start(bf16[1500,512]{0,1:T(8,128)(2,1)} %copy.103) | copy-start | bytes 4608004
  232.9 20.4 %collective-permute-start.7 = (bf16[448,1024]{1,0:T(8,128)(2,1)}, bf16[448,1024]{1,0:T(8,128)(2,1)}, u32[]{:S(2)}, u32[]{:S(2)}) collective-permute-start(bf16[448,1024]{1,0:T(8,128)(2,1)} %convolution_convert_fusion.10), channel_id=1, source_target_pairs={{0,1},{1,0},{2,3},{3,2},{4,5},{5,4},{6,7},{7,6},{8,9},{9,8},{10,11... | collective-permute-start | bytes 2752520 | tf_op jit(solution)/shard_map/ppermute | solution.py:92
  284.8 19.5 %collective-permute-start.3 = (bf16[448,1024]{1,0:T(8,128)(2,1)}, bf16[448,1024]{1,0:T(8,128)(2,1)}, u32[]{:S(2)}, u32[]{:S(2)}) collective-permute-start(bf16[448,1024]{1,0:T(8,128)(2,1)} %convolution_convert_fusion.12), channel_id=1, source_target_pairs={{0,1},{1,0},{2,3},{3,2},{4,5},{5,4},{6,7},{7,6},{8,9},{9,8},{10,11... | collective-permute-start | bytes 2752520 | tf_op jit(solution)/shard_map/ppermute | solution.py:92
  336.2 18.5 %copy-start.9 = (f32[448,1024]{1,0:T(8,128)S(1)}, f32[448,1024]{1,0:T(8,128)}, u32[]{:S(2)}) copy-start(f32[448,1024]{1,0:T(8,128)} %copy-done.8) | copy-start | bytes 5505028
  336.2 18.4 %collective-permute-start.4 = (bf16[448,1024]{1,0:T(8,128)(2,1)S(1)}, bf16[448,1024]{1,0:T(8,128)(2,1)S(1)}, u32[]{:S(2)}, u32[]{:S(2)}) collective-permute-start(bf16[448,1024]{1,0:T(8,128)(2,1)S(1)} %convolution_convert_fusion.11), channel_id=1, source_target_pairs={{0,1},{1,0},{2,3},{3,2},{4,5},{5,4},{6,7},{7,6},{8,9},{9,8},{10,11... | collective-permute-start | bytes 2752520 | tf_op jit(solution)/shard_map/ppermute | solution.py:92
  366.5 23.3 %collective-permute-start.9 = (bf16[448,1024]{1,0:T(8,128)(2,1)S(1)}, bf16[448,1024]{1,0:T(8,128)(2,1)S(1)}, u32[]{:S(2)}, u32[]{:S(2)}) collective-permute-start(bf16[448,1024]{1,0:T(8,128)(2,1)S(1)} %convolution_convert_fusion.15), channel_id=1, source_target_pairs={{0,1},{1,0},{2,3},{3,2},{4,5},{5,4},{6,7},{7,6},{8,9},{9,8},{10,11... | collective-permute-start | bytes 2752520 | tf_op jit(solution)/shard_map/ppermute | solution.py:92
  370.0 33.7 %collective-permute-start.5 = (bf16[448,1024]{1,0:T(8,128)(2,1)S(1)}, bf16[448,1024]{1,0:T(8,128)(2,1)S(1)}, u32[]{:S(2)}, u32[]{:S(2)}) collective-permute-start(bf16[448,1024]{1,0:T(8,128)(2,1)S(1)} %convolution_convert_fusion.17), channel_id=1, source_target_pairs={{0,1},{1,0},{2,3},{3,2},{4,5},{5,4},{6,7},{7,6},{8,9},{9,8},{10,11... | collective-permute-start | bytes 2752520 | tf_op jit(solution)/shard_map/ppermute | solution.py:92
  414.1 154.7 %reduce-scatter.23.cloned.1.call-start = ((), (), s32[]{:S(2)}) async-start(), calls=%async_computation.22 | async-start | bytes 1114112 | tf_op jit(solution)/shard_map/reduce_scatter | solution.py:97
  450.4 142.3 %reduce-scatter.21.cloned.1.call-start = ((), (), s32[]{:S(2)}) async-start(), calls=%async_computation.20 | async-start | bytes 1114112 | tf_op jit(solution)/shard_map/reduce_scatter | solution.py:97
  450.9 15.0 %copy-start.41 = (bf16[448,512]{0,1:T(8,128)(2,1)S(1)}, bf16[448,512]{0,1:T(8,128)(2,1)}, u32[]{:S(2)}) copy-start(bf16[448,512]{0,1:T(8,128)(2,1)} %copy.110) | copy-start | bytes 1376260
  479.1 173.8 %reduce-scatter.19.cloned.1.call-start = ((), (), s32[]{:S(2)}) async-start(), calls=%async_computation.18 | async-start | bytes 1114112 | tf_op jit(solution)/shard_map/reduce_scatter | solution.py:97
  489.0 16.9 %collective-permute-start.10 = (bf16[448,1024]{1,0:T(8,128)(2,1)}, bf16[448,1024]{1,0:T(8,128)(2,1)}, u32[]{:S(2)}, u32[]{:S(2)}) collective-permute-start(bf16[448,1024]{1,0:T(8,128)(2,1)} %convolution_convert_fusion.9), channel_id=1, source_target_pairs={{0,1},{1,0},{2,3},{3,2},{4,5},{5,4},{6,7},{7,6},{8,9},{9,8},{10,11... | collective-permute-start | bytes 2752520 | tf_op jit(solution)/shard_map/ppermute | solution.py:92
  499.1 214.0 %reduce-scatter.15.cloned.1.call-start = ((), (), s32[]{:S(2)}) async-start(), calls=%async_computation.14 | async-start | bytes 1114112 | tf_op jit(solution)/shard_map/reduce_scatter | solution.py:97
  522.5 250.7 %reduce-scatter.17.cloned.1.call-start = ((), (), s32[]{:S(2)}) async-start(), calls=%async_computation.16 | async-start | bytes 1114112 | tf_op jit(solution)/shard_map/reduce_scatter | solution.py:97
  525.6 13.2 copy-start.73
  527.9 306.1 %reduce-scatter.11.cloned.1.call-start = ((), (), s32[]{:S(2)}) async-start(), calls=%async_computation.10 | async-start | bytes 1114112 | tf_op jit(solution)/shard_map/reduce_scatter | solution.py:97
  542.2 352.6 %reduce-scatter.13.cloned.1.call-start = ((), (), s32[]{:S(2)}) async-start(), calls=%async_computation.12 | async-start | bytes 1114112 | tf_op jit(solution)/shard_map/reduce_scatter | solution.py:97
  550.0 421.1 %reduce-scatter.29.cloned.1.call-start = ((), (), s32[]{:S(2)}) async-start(), calls=%async_computation.28 | async-start | bytes 4456448 | tf_op jit(solution)/shard_map/reduce_scatter | solution.py:97
  558.4 488.8 %reduce-scatter.27.cloned.1.call-start = ((), (), s32[]{:S(2)}) async-start(), calls=%async_computation.26 | async-start | bytes 4456448 | tf_op jit(solution)/shard_map/reduce_scatter | solution.py:97
  568.0 403.6 %copy-start.18 = (bf16[8,64,1500]{2,1,0:T(8,128)(2,1)S(1)}, bf16[8,64,1500]{2,1,0:T(8,128)(2,1)}, u32[]{:S(2)}) copy-start(bf16[8,64,1500]{2,1,0:T(8,128)(2,1)} %fusion.32) | copy-start | bytes 4608004
  568.0 608.8 %all-gather.25.cloned.1.call-start = ((), (), s32[]{:S(2)}) async-start(), calls=%async_computation.25 | async-start | bytes 1114112 | tf_op jit(solution)/shard_map/all_gather | solution.py:98
  568.8 610.9 %all-gather.23.cloned.1.call-start = ((), (), s32[]{:S(2)}) async-start(), calls=%async_computation.23 | async-start | bytes 1114112 | tf_op jit(solution)/shard_map/all_gather | solution.py:98
  569.3 613.2 %all-gather.21.cloned.1.call-start = ((), (), s32[]{:S(2)}) async-start(), calls=%async_computation.21 | async-start | bytes 1114112 | tf_op jit(solution)/shard_map/all_gather | solution.py:98
  592.8 610.5 %all-gather.19.cloned.1.call-start = ((), (), s32[]{:S(2)}) async-start(), calls=%async_computation.19 | async-start | bytes 1114112 | tf_op jit(solution)/shard_map/all_gather | solution.py:98
  652.9 589.3 %all-gather.15.cloned.1.call-start = ((), (), s32[]{:S(2)}) async-start(), calls=%async_computation.15 | async-start | bytes 1114112 | tf_op jit(solution)/shard_map/all_gather | solution.py:98
  713.0 568.0 %all-gather.17.cloned.1.call-start = ((), (), s32[]{:S(2)}) async-start(), calls=%async_computation.17 | async-start | bytes 1114112 | tf_op jit(solution)/shard_map/all_gather | solution.py:98
  773.2 546.7 %all-gather.11.cloned.1.call-start = ((), (), s32[]{:S(2)}) async-start(), calls=%async_computation.11 | async-start | bytes 1114112 | tf_op jit(solution)/shard_map/all_gather | solution.py:98
  834.0 524.8 %all-gather.13.cloned.1.call-start = ((), (), s32[]{:S(2)}) async-start(), calls=%async_computation.13 | async-start | bytes 1114112 | tf_op jit(solution)/shard_map/all_gather | solution.py:98
  894.8 515.5 %all-gather.29.cloned.1.call-start = ((), (), s32[]{:S(2)}) async-start(), calls=%async_computation.29 | async-start | bytes 4456448 | tf_op jit(solution)/shard_map/all_gather | solution.py:98
  971.1 490.2 %all-gather.27.cloned.1.call-start = ((), (), s32[]{:S(2)}) async-start(), calls=%async_computation.27 | async-start | bytes 4456448 | tf_op jit(solution)/shard_map/all_gather | solution.py:98
  975.5 36.9 %collective-permute-start.12 = (bf16[1500,512]{1,0:T(8,128)(2,1)}, bf16[1500,512]{1,0:T(8,128)(2,1)}, u32[]{:S(2)}, u32[]{:S(2)}) collective-permute-start(bf16[1500,512]{1,0:T(8,128)(2,1)} %fusion.36), channel_id=1, source_target_pairs={{0,1},{1,0},{2,3},{3,2},{4,5},{5,4},{6,7},{7,6},{8,9},{9,8},{10,11... | collective-permute-start | bytes 4608008 | tf_op jit(solution)/shard_map/ppermute | solution.py:294
  981.1 31.3 %copy-start.32 = (bf16[8,64,1500]{2,1,0:T(8,128)(2,1)S(1)}, bf16[8,64,1500]{2,1,0:T(8,128)(2,1)}, u32[]{:S(2)}) copy-start(bf16[8,64,1500]{2,1,0:T(8,128)(2,1)} %get-tuple-element.188) | copy-start | bytes 4608004
  981.1 31.3 %copy-start.60 = (bf16[1024,512]{1,0:T(8,128)(2,1)S(1)}, bf16[1024,512]{1,0:T(8,128)(2,1)}, u32[]{:S(2)}) copy-start(bf16[1024,512]{1,0:T(8,128)(2,1)} %param.44) | copy-start | bytes 3145732
  982.8 33.7 %copy-start.20 = (bf16[8,64,1500]{2,1,0:T(8,128)(2,1)S(1)}, bf16[8,64,1500]{2,1,0:T(8,128)(2,1)}, u32[]{:S(2)}) copy-start(bf16[8,64,1500]{2,1,0:T(8,128)(2,1)} %copy-done.19) | copy-start | bytes 4608004
  982.8 123.6 %collective-permute-start.8 = (bf16[448,1024]{1,0:T(8,128)(2,1)}, bf16[448,1024]{1,0:T(8,128)(2,1)}, u32[]{:S(2)}, u32[]{:S(2)}) collective-permute-start(bf16[448,1024]{1,0:T(8,128)(2,1)} %add_convert_fusion.1), channel_id=1, source_target_pairs={{0,1},{1,0},{2,3},{3,2},{4,5},{5,4},{6,7},{7,6},{8,9},{9,8},{10,11... | collective-permute-start | bytes 2752520 | tf_op jit(solution)/shard_map/ppermute | solution.py:92
  1052.0 36.9 %collective-permute-start.13 = (bf16[1500,512]{1,0:T(8,128)(2,1)}, bf16[1500,512]{1,0:T(8,128)(2,1)}, u32[]{:S(2)}, u32[]{:S(2)}) collective-permute-start(bf16[1500,512]{1,0:T(8,128)(2,1)} %fusion.37), channel_id=1, source_target_pairs={{0,1},{1,0},{2,3},{3,2},{4,5},{5,4},{6,7},{7,6},{8,9},{9,8},{10,11... | collective-permute-start | bytes 4608008 | tf_op jit(solution)/shard_map/ppermute | solution.py:294
  1060.7 45.8 %collective-permute-start.11 = (bf16[448,1024]{1,0:T(8,128)(2,1)}, bf16[448,1024]{1,0:T(8,128)(2,1)}, u32[]{:S(2)}, u32[]{:S(2)}) collective-permute-start(bf16[448,1024]{1,0:T(8,128)(2,1)} %add_convert_fusion), channel_id=1, source_target_pairs={{0,1},{1,0},{2,3},{3,2},{4,5},{5,4},{6,7},{7,6},{8,9},{9,8},{10,11... | collective-permute-start | bytes 2752520 | tf_op jit(solution)/shard_map/ppermute | solution.py:92
  1061.3 27.6 %copy-start.34 = (bf16[8,64,1500]{2,1,0:T(8,128)(2,1)S(1)}, bf16[8,64,1500]{2,1,0:T(8,128)(2,1)}, u32[]{:S(2)}) copy-start(bf16[8,64,1500]{2,1,0:T(8,128)(2,1)} %copy-done.33) | copy-start | bytes 4608004
  (160 other events, 653.6 us)
Sparse Core Ops, SparseCore 0:
  414.3 57.9 reduce-scatter.24
  475.8 56.7 reduce-scatter.22
  536.3 56.4 reduce-scatter.20
  596.2 56.6 reduce-scatter.18
  656.3 56.6 reduce-scatter.14
  716.5 56.6 reduce-scatter.16
  777.4 56.6 reduce-scatter.10
  838.2 56.5 reduce-scatter.12
  899.2 71.8 reduce-scatter.28
  975.4 71.8 reduce-scatter.26
  1049.4 36.9 all-gather.24
  1088.4 36.8 all-gather.22
  1127.5 36.8 all-gather.20
  1166.4 36.7 all-gather.18
  1205.3 36.8 all-gather.14
  1244.2 36.8 all-gather.16
  1283.1 36.8 all-gather.10
  1321.9 36.8 all-gather.12
  1361.0 49.3 all-gather.28
  1412.4 48.8 all-gather.26
where the time goes:
time: 1480 us; the launch traced here: 1470 us
  waiting for transfers between devices  843 us (57%)
  matrix products  294 us (20%)
  other arithmetic  140 us (9%)
  local copies, waits for them, and re-layouts  105 us (7%)
  blocking collectives  57.9 us (4%)
  starting transfers between devices  17.7 us (1%)
  between operations  16.5 us (1%)
    reduce_scatter x10, waiting for transfers between devices, dp_sum(): share = lax.psum_scatter(grads, 'dp', scatter_dimension=0, tiled=True)  429 us
    all_gather x10, waiting for transfers between devices, dp_sum(): return lax.all_gather(share, 'dp', axis=0, tiled=True)  255 us
    ppermute x12, waiting for transfers between devices, tensor_sum(): other = lax.ppermute(mine, 'tensor', [(0, 1), (1, 0)])  103 us
    psum x1, blocking collectives, local(): summed = lax.psum(jnp.concatenate(vectors), 'dp')  57.9 us
    ppermute x2, waiting for transfers between devices, local(): other = lax.ppermute(terms(1 - me).astype(BF16), 'tensor', [(0, 1), (1, 0)])  54 us
    dot_general x24, matrix products, project_back(): return jnp.einsum('lc,dc->ld', grads, weight, preferred_element_type=F32)  53.9 us
    unnamed x353, local copies, waits for them, and re-layouts  52.1 us
    dot_general x20, matrix products, project(): return jnp.dot(inputs, weight, preferred_element_type=F32)  51.3 us
  transfers between devices with their start and end apart: 34, of which 26 were waited for; matrix products, arithmetic and copies ran while one was open for 20% of the time, Pallas kernels for 0%

commit v1 on v0

--- a/solution.py
+++ b/solution.py
@@ -8,6 +8,27 @@
 EPSILON = 1e-05
 F32 = jnp.float32
 BF16 = jnp.bfloat16
+
+
+def joined_along(tiles, dim):
+    shape = list(tiles.shape[1:])
+    shape[dim] *= tiles.shape[0]
+    return jnp.moveaxis(tiles, 0, dim).reshape(shape)
+
+
+def doubled(value, axis):
+    length, index = (lax.axis_size(axis), lax.axis_index(axis))
+    blocks, bit = (value[None], 1)
+    while bit < length:
+        other = lax.ppermute(blocks, axis, [(i, i ^ bit) for i in range(length)])
+        low = index & bit == 0
+        blocks = jnp.concatenate([jnp.where(low, blocks, other), jnp.where(low, other, blocks)])
+        bit *= 2
+    return blocks
+
+
+def doubled_up(x, axis, dim):
+    return joined_along(doubled(x, axis), dim)
 
 
 def normalize(values, norm_gain, norm_shift):
@@ -95,7 +116,7 @@
 
 def dp_sum(grads):
     share = lax.psum_scatter(grads, "dp", scatter_dimension=0, tiled=True)
-    return lax.all_gather(share, "dp", axis=0, tiled=True)
+    return doubled_up(share, "dp", 0)
 
 
 def local(

time: 1480 us -> 1420 us (0.959)
  waiting for transfers between devices: 843 us -> 695 us
  starting transfers between devices: 17.7 us -> 54.9 us
  other arithmetic: 140 us -> 173 us
    all_gather x10 -> x0, waiting for transfers between devices: 255 us -> none  [dp_sum(): return lax.all_gather(share, 'dp', axis=0, tiled=True)]
    ppermute x0 -> x40, waiting for transfers between devices: none -> 233 us  [doubled(): other = lax.ppermute(blocks, axis, [(i, i ^ bit) for i in range(length)])]
    reduce_scatter x10, waiting for transfers between devices: 429 us -> 304 us  [dp_sum(): share = lax.psum_scatter(grads, 'dp', scatter_dimension=0, tiled=True)]
    ppermute x0 -> x40, starting transfers between devices: none -> 37.5 us  [doubled(): other = lax.ppermute(blocks, axis, [(i, i ^ bit) for i in range(length)])]
    select_n x0 -> x40, other arithmetic: none -> 20.6 us  [doubled(): jnp.where(low, blocks, other)]
    unnamed x353 -> x397, local copies, waits for them, and re-layouts: 52.1 us -> 58.3 us
  transfers between devices with their start and end apart: 34 -> 64, of which waited for: 26 -> 29; matrix products, arithmetic and copies ran while one was open for 20% -> 24% of each run, Pallas kernels for 0% -> 0%
where the time goes in v1:
time: 1420 us; the launch traced here: 1410 us
  waiting for transfers between devices  695 us (49%)
  matrix products  294 us (21%)
  other arithmetic  173 us (12%)
  local copies, waits for them, and re-layouts  114 us (8%)
  blocking collectives  61.2 us (4%)
  starting transfers between devices  54.9 us (4%)
  between operations  16.9 us (1%)
    reduce_scatter x10, waiting for transfers between devices, dp_sum(): share = lax.psum_scatter(grads, 'dp', scatter_dimension=0, tiled=True)  304 us
    ppermute x40, waiting for transfers between devices, doubled(): other = lax.ppermute(blocks, axis, [(i, i ^ bit) for i in range(length)])  233 us
    ppermute x12, waiting for transfers between devices, tensor_sum(): other = lax.ppermute(mine, 'tensor', [(0, 1), (1, 0)])  106 us
    psum x1, blocking collectives, local(): summed = lax.psum(jnp.concatenate(vectors), 'dp')  61.2 us
    unnamed x397, local copies, waits for them, and re-layouts  58.3 us
    dot_general x24, matrix products, project_back(): return jnp.einsum('lc,dc->ld', grads, weight, preferred_element_type=F32)  52.9 us
    dot_general x20, matrix products, project(): return jnp.dot(inputs, weight, preferred_element_type=F32)  51.3 us
    ppermute x2, waiting for transfers between devices, local(): other = lax.ppermute(terms(1 - me).astype(BF16), 'tensor', [(0, 1), (1, 0)])  51.1 us
  transfers between devices with their start and end apart: 64, of which 29 were waited for; matrix products, arithmetic and copies ran while one was open for 24% of the time, Pallas kernels for 0%

profile of v1, /device:TPU:0, one launch (start us, length us, event | category | flops | bytes accessed | tf_op | source)
XLA Modules:
  0.0 1407.6 jit_solution(3977421016702597206)
XLA Ops:
  41.5 9.8 fusion.219
  51.3 8.0 copy_bitcast_fusion
  86.3 6.1 exponential_reduce_fusion.1
  93.6 12.4 fusion.135
  108.4 21.7 %collective-permute-done.1 = bf16[448,1024]{1,0:T(8,128)(2,1)S(1)} collective-permute-done((bf16[448,1024]{1,0:T(8,128)(2,1)S(1)}, bf16[448,1024]{1,0:T(8,128)(2,1)S(1)}, u32[]{:S(2)}, u32[]{:S(2)}) %collective-permute-start.1) | collective-permute-done | bytes 917536 | tf_op jit(solution)/shard_map/ppermute | solution.py:113
  151.9 15.1 %collective-permute-done.6 = bf16[448,1024]{1,0:T(8,128)(2,1)} collective-permute-done((bf16[448,1024]{1,0:T(8,128)(2,1)}, bf16[448,1024]{1,0:T(8,128)(2,1)}, u32[]{:S(2)}, u32[]{:S(2)}) %collective-permute-start.6) | collective-permute-done | bytes 917536 | tf_op jit(solution)/shard_map/ppermute | solution.py:113
  170.6 13.8 collective-permute-done.2
  194.6 15.2 %multiply_reduce_fusion.1 = (f32[8,448]{1,0:T(8,128)S(1)}, f32[8,448,1500]{2,1,0:T(8,128)}) fusion(f32[8,448,1500]{2,1,0:T(8,128)} %copy-done.1, f32[8,448]{1,0:T(8,128)S(1)} %log_add_fusion.2, bf16[448,8,64]{0,2,1:T(8,128)(2,1)} %bitcast.396, bf16[1500,8,64]{0,2,1:T(8,128)(2,1)} %bitcast.385), kind=kOutput, calls=%fused_computation.3 | convolution fusion | flops 709628416 | bytes 45031424 | tf_op jit(solution)/shard_map/lhe,khe->hlk/dot_general | solution.py:76
  209.8 15.1 %multiply_convert_fusion.1 = bf16[8,448,1500]{2,1,0:T(8,128)(2,1)S(1)} fusion(f32[8,448,1500]{2,1,0:T(8,128)} %get-tuple-element.245, f32[8,448,1500]{2,1,0:T(8,128)} %copy-done.1, f32[8,448]{1,0:T(8,128)S(1)} %get-tuple-element.244, f32[8,448]{1,0:T(8,128)S(1)} %log_add_fusion.2), kind=kLoop, calls=%fused_computation.2 | loop fusion | flops 26880000 | bytes 53788672 | tf_op jit(solution)/shard_map/convert_element_type | solution.py:78
  241.9 5.5 fusion.222
  247.5 5.9 collective-permute-done.7
  265.2 9.0 multiply_reduce_fusion.5
  274.9 5.5 multiply_convert_fusion.3
  291.5 5.0 fusion.35
  299.2 5.5 collective-permute-done.3
  314.7 5.7 exponential_reduce_fusion
  322.5 10.1 fusion.138
  335.8 10.9 convert_reduce_fusion.3
  346.8 6.4 collective-permute-done.4
  372.5 15.9 %collective-permute-done.9 = bf16[448,1024]{1,0:T(8,128)(2,1)S(1)} collective-permute-done((bf16[448,1024]{1,0:T(8,128)(2,1)S(1)}, bf16[448,1024]{1,0:T(8,128)(2,1)S(1)}, u32[]{:S(2)}, u32[]{:S(2)}) %collective-permute-start.9) | collective-permute-done | bytes 917536 | tf_op jit(solution)/shard_map/ppermute | solution.py:113
  389.9 12.5 collective-permute-done.5
  415.2 12.0 convert_reduce_fusion.2
  428.3 5.5 fusion.113
  433.8 15.4 %multiply_reduce_fusion = (f32[8,448]{1,0:T(8,128)S(1)}, f32[8,448,1500]{2,1,0:T(8,128)}) fusion(f32[8,448,1500]{2,1,0:T(8,128)} %copy-done.2, f32[8,448]{1,0:T(8,128)S(1)} %log_add_fusion, bf16[448,8,64]{0,2,1:T(8,128)(2,1)} %bitcast.399, bf16[1500,8,64]{0,2,1:T(8,128)(2,1)} %bitcast.382), kind=kOutput, calls=%fused_computation.1 | convolution fusion | flops 709628416 | bytes 45031424 | tf_op jit(solution)/shard_map/lhe,khe->hlk/dot_general | solution.py:76
  449.4 14.9 %multiply_convert_fusion = bf16[8,448,1500]{2,1,0:T(8,128)(2,1)S(1)} fusion(f32[8,448,1500]{2,1,0:T(8,128)} %get-tuple-element.252, f32[8,448,1500]{2,1,0:T(8,128)} %copy-done.2, f32[8,448]{1,0:T(8,128)S(1)} %get-tuple-element.251, f32[8,448]{1,0:T(8,128)S(1)} %log_add_fusion), kind=kLoop, calls=%fused_computation | loop fusion | flops 26880000 | bytes 53788672 | tf_op jit(solution)/shard_map/convert_element_type | solution.py:78
  472.2 5.4 fusion.110
  477.6 8.1 convert_reduce_fusion.8
  495.5 8.9 collective-permute-done.10
  514.8 5.9 convert_reduce_fusion.11
  521.6 5.2 convert_reduce_fusion.10
  552.5 8.9 convolution_convert_fusion.1
  573.8 28.4 %collective-permute-done.12 = bf16[1500,512]{1,0:T(8,128)(2,1)S(1)} collective-permute-done((bf16[1500,512]{1,0:T(8,128)(2,1)S(1)}, bf16[1500,512]{1,0:T(8,128)(2,1)S(1)}, u32[]{:S(2)}, u32[]{:S(2)}) %collective-permute-start.12) | collective-permute-done | bytes 1536032 | tf_op jit(solution)/shard_map/ppermute | solution.py:315
  605.0 6.2 convolution_convert_fusion
  634.9 22.7 %collective-permute-done.13 = bf16[1500,512]{1,0:T(8,128)(2,1)} collective-permute-done((bf16[1500,512]{1,0:T(8,128)(2,1)}, bf16[1500,512]{1,0:T(8,128)(2,1)}, u32[]{:S(2)}, u32[]{:S(2)}) %collective-permute-start.13) | collective-permute-done | bytes 1536032 | tf_op jit(solution)/shard_map/ppermute | solution.py:315
  665.3 12.9 copy.122
  718.5 61.2 %psum.7 = f32[13312]{0:T(1024)} all-reduce(f32[13312]{0:T(1024)} %add_dynamic-update-slice_fusion), channel_id=1, replica_groups=mesh['dp'=16,'tensor'=2] {'dp'}, use_global_device_ids=true, to_apply=%region_64.65 | all-reduce | flops 13312 | bytes 106496 | tf_op jit(solution)/shard_map/psum | solution.py:348
  803.1 96.1 %reduce-scatter.11.cloned.1.call-done = bf16[64,512]{1,0:T(8,128)(2,1)} async-done(((bf16[1024,512]{1,0:T(8,128)(2,1)}), bf16[64,512]{1,0:T(8,128)(2,1)}) %reduce-scatter.11.cloned.1.call-update) | async-done | bytes 65552 | tf_op jit(solution)/shard_map/reduce_scatter | solution.py:118
  900.2 59.4 %reduce-scatter.13.cloned.1.call-done = bf16[64,512]{1,0:T(8,128)(2,1)} async-done(((bf16[1024,512]{1,0:T(8,128)(2,1)}), bf16[64,512]{1,0:T(8,128)(2,1)}) %reduce-scatter.13.cloned.1.call-update) | async-done | bytes 65552 | tf_op jit(solution)/shard_map/reduce_scatter | solution.py:118
  982.4 14.4 %collective-permute-done.24 = bf16[4,64,512]{2,1,0:T(8,128)(2,1)S(1)} collective-permute-done((bf16[4,64,512]{2,1,0:T(8,128)(2,1)S(1)}, bf16[4,64,512]{2,1,0:T(8,128)(2,1)S(1)}, u32[]{:S(2)}, u32[]{:S(2)}) %collective-permute-start.24) | collective-permute-done | bytes 262176 | tf_op jit(solution)/shard_map/ppermute | solution.py:23
  1000.8 19.1 %collective-permute-done.16 = bf16[4,64,512]{2,1,0:T(8,128)(2,1)S(1)} collective-permute-done((bf16[4,64,512]{2,1,0:T(8,128)(2,1)S(1)}, bf16[4,64,512]{2,1,0:T(8,128)(2,1)S(1)}, u32[]{:S(2)}, u32[]{:S(2)}) %collective-permute-start.16) | collective-permute-done | bytes 262176 | tf_op jit(solution)/shard_map/ppermute | solution.py:23
  1021.5 6.9 collective-permute-done.20
  1030.9 59.8 %reduce-scatter.27.cloned.1.call-done = bf16[64,2048]{1,0:T(8,128)(2,1)} async-done(((bf16[1024,2048]{1,0:T(8,128)(2,1)}), bf16[64,2048]{1,0:T(8,128)(2,1)}) %reduce-scatter.27.cloned.1.call-update) | async-done | bytes 262160 | tf_op jit(solution)/shard_map/reduce_scatter | solution.py:118
  1095.7 89.1 %reduce-scatter.29.cloned.1.call-done = bf16[128,1024]{1,0:T(8,128)(2,1)} async-done(((bf16[2048,1024]{1,0:T(8,128)(2,1)}), bf16[128,1024]{1,0:T(8,128)(2,1)}) %reduce-scatter.29.cloned.1.call-update) | async-done | bytes 262160 | tf_op jit(solution)/shard_map/reduce_scatter | solution.py:118
  1191.2 10.1 collective-permute-done.51
  1201.3 10.4 collective-permute-done.48
  1220.0 60.6 %collective-permute-done.52 = bf16[4,128,1024]{2,1,0:T(8,128)(2,1)S(1)} collective-permute-done((bf16[4,128,1024]{2,1,0:T(8,128)(2,1)S(1)}, bf16[4,128,1024]{2,1,0:T(8,128)(2,1)S(1)}, u32[]{:S(2)}, u32[]{:S(2)}) %collective-permute-start.52) | collective-permute-done | bytes 1048608 | tf_op jit(solution)/shard_map/ppermute | solution.py:23
  1285.7 64.7 %collective-permute-done.49 = bf16[8,64,2048]{2,1,0:T(8,128)(2,1)S(1)} collective-permute-done((bf16[8,64,2048]{2,1,0:T(8,128)(2,1)S(1)}, bf16[8,64,2048]{2,1,0:T(8,128)(2,1)S(1)}, u32[]{:S(2)}, u32[]{:S(2)}) %collective-permute-start.49) | collective-permute-done | bytes 2097184 | tf_op jit(solution)/shard_map/ppermute | solution.py:23
  1355.8 39.2 %collective-permute-done.53 = bf16[8,128,1024]{2,1,0:T(8,128)(2,1)S(1)} collective-permute-done((bf16[8,128,1024]{2,1,0:T(8,128)(2,1)S(1)}, bf16[8,128,1024]{2,1,0:T(8,128)(2,1)S(1)}, u32[]{:S(2)}, u32[]{:S(2)}) %collective-permute-start.53) | collective-permute-done | bytes 2097184 | tf_op jit(solution)/shard_map/ppermute | solution.py:23
  (781 shorter events, 424.2 us)
Async XLA Ops:
  7.2 654.5 %reduce-scatter.25.cloned.1.call-start = ((), (), s32[]{:S(2)}) async-start(), calls=%async_computation.17 | async-start | bytes 1114112 | tf_op jit(solution)/shard_map/reduce_scatter | solution.py:118
  38.4 35.6 %collective-permute-start = (bf16[448,1024]{1,0:T(8,128)(2,1)}, bf16[448,1024]{1,0:T(8,128)(2,1)}, u32[]{:S(2)}, u32[]{:S(2)}) collective-permute-start(bf16[448,1024]{1,0:T(8,128)(2,1)} %convolution_convert_fusion.14), channel_id=1, source_target_pairs={{0,1},{1,0},{2,3},{3,2},{4,5},{5,4},{6,7},{7,6},{8,9},{9,8},{10,11... | collective-permute-start | bytes 2752520 | tf_op jit(solution)/shard_map/ppermute | solution.py:113
  108.2 21.9 %collective-permute-start.1 = (bf16[448,1024]{1,0:T(8,128)(2,1)S(1)}, bf16[448,1024]{1,0:T(8,128)(2,1)S(1)}, u32[]{:S(2)}, u32[]{:S(2)}) collective-permute-start(bf16[448,1024]{1,0:T(8,128)(2,1)S(1)} %convolution_convert_fusion.13), channel_id=1, source_target_pairs={{0,1},{1,0},{2,3},{3,2},{4,5},{5,4},{6,7},{7,6},{8,9},{9,8},{10,11... | collective-permute-start | bytes 2752520 | tf_op jit(solution)/shard_map/ppermute | solution.py:113
  143.5 23.5 %collective-permute-start.6 = (bf16[448,1024]{1,0:T(8,128)(2,1)}, bf16[448,1024]{1,0:T(8,128)(2,1)}, u32[]{:S(2)}, u32[]{:S(2)}) collective-permute-start(bf16[448,1024]{1,0:T(8,128)(2,1)} %convolution_convert_fusion.16), channel_id=1, source_target_pairs={{0,1},{1,0},{2,3},{3,2},{4,5},{5,4},{6,7},{7,6},{8,9},{9,8},{10,11... | collective-permute-start | bytes 2752520 | tf_op jit(solution)/shard_map/ppermute | solution.py:113
  146.8 37.7 %collective-permute-start.2 = (bf16[448,1024]{1,0:T(8,128)(2,1)}, bf16[448,1024]{1,0:T(8,128)(2,1)}, u32[]{:S(2)}, u32[]{:S(2)}) collective-permute-start(bf16[448,1024]{1,0:T(8,128)(2,1)} %convolution_convert_fusion.18), channel_id=1, source_target_pairs={{0,1},{1,0},{2,3},{3,2},{4,5},{5,4},{6,7},{7,6},{8,9},{9,8},{10,11... | collective-permute-start | bytes 2752520 | tf_op jit(solution)/shard_map/ppermute | solution.py:113
  233.0 20.4 %collective-permute-start.7 = (bf16[448,1024]{1,0:T(8,128)(2,1)}, bf16[448,1024]{1,0:T(8,128)(2,1)}, u32[]{:S(2)}, u32[]{:S(2)}) collective-permute-start(bf16[448,1024]{1,0:T(8,128)(2,1)} %convolution_convert_fusion.10), channel_id=1, source_target_pairs={{0,1},{1,0},{2,3},{3,2},{4,5},{5,4},{6,7},{7,6},{8,9},{9,8},{10,11... | collective-permute-start | bytes 2752520 | tf_op jit(solution)/shard_map/ppermute | solution.py:113
  285.2 19.6 %collective-permute-start.3 = (bf16[448,1024]{1,0:T(8,128)(2,1)}, bf16[448,1024]{1,0:T(8,128)(2,1)}, u32[]{:S(2)}, u32[]{:S(2)}) collective-permute-start(bf16[448,1024]{1,0:T(8,128)(2,1)} %convolution_convert_fusion.12), channel_id=1, source_target_pairs={{0,1},{1,0},{2,3},{3,2},{4,5},{5,4},{6,7},{7,6},{8,9},{9,8},{10,11... | collective-permute-start | bytes 2752520 | tf_op jit(solution)/shard_map/ppermute | solution.py:113
  334.7 18.5 %collective-permute-start.4 = (bf16[448,1024]{1,0:T(8,128)(2,1)S(1)}, bf16[448,1024]{1,0:T(8,128)(2,1)S(1)}, u32[]{:S(2)}, u32[]{:S(2)}) collective-permute-start(bf16[448,1024]{1,0:T(8,128)(2,1)S(1)} %convolution_convert_fusion.11), channel_id=1, source_target_pairs={{0,1},{1,0},{2,3},{3,2},{4,5},{5,4},{6,7},{7,6},{8,9},{9,8},{10,11... | collective-permute-start | bytes 2752520 | tf_op jit(solution)/shard_map/ppermute | solution.py:113
  365.1 23.3 %collective-permute-start.9 = (bf16[448,1024]{1,0:T(8,128)(2,1)S(1)}, bf16[448,1024]{1,0:T(8,128)(2,1)S(1)}, u32[]{:S(2)}, u32[]{:S(2)}) collective-permute-start(bf16[448,1024]{1,0:T(8,128)(2,1)S(1)} %convolution_convert_fusion.15), channel_id=1, source_target_pairs={{0,1},{1,0},{2,3},{3,2},{4,5},{5,4},{6,7},{7,6},{8,9},{9,8},{10,11... | collective-permute-start | bytes 2752520 | tf_op jit(solution)/shard_map/ppermute | solution.py:113
  368.6 33.8 %collective-permute-start.5 = (bf16[448,1024]{1,0:T(8,128)(2,1)S(1)}, bf16[448,1024]{1,0:T(8,128)(2,1)S(1)}, u32[]{:S(2)}, u32[]{:S(2)}) collective-permute-start(bf16[448,1024]{1,0:T(8,128)(2,1)S(1)} %convolution_convert_fusion.17), channel_id=1, source_target_pairs={{0,1},{1,0},{2,3},{3,2},{4,5},{5,4},{6,7},{7,6},{8,9},{9,8},{10,11... | collective-permute-start | bytes 2752520 | tf_op jit(solution)/shard_map/ppermute | solution.py:113
  412.7 265.5 %reduce-scatter.23.cloned.1.call-start = ((), (), s32[]{:S(2)}) async-start(), calls=%async_computation.16 | async-start | bytes 1114112 | tf_op jit(solution)/shard_map/reduce_scatter | solution.py:118
  449.2 229.6 %reduce-scatter.21.cloned.1.call-start = ((), (), s32[]{:S(2)}) async-start(), calls=%async_computation.15 | async-start | bytes 1114112 | tf_op jit(solution)/shard_map/reduce_scatter | solution.py:118
  477.6 201.3 %reduce-scatter.19.cloned.1.call-start = ((), (), s32[]{:S(2)}) async-start(), calls=%async_computation.14 | async-start | bytes 1114112 | tf_op jit(solution)/shard_map/reduce_scatter | solution.py:118
  487.5 16.9 %collective-permute-start.10 = (bf16[448,1024]{1,0:T(8,128)(2,1)}, bf16[448,1024]{1,0:T(8,128)(2,1)}, u32[]{:S(2)}, u32[]{:S(2)}) collective-permute-start(bf16[448,1024]{1,0:T(8,128)(2,1)} %convolution_convert_fusion.9), channel_id=1, source_target_pairs={{0,1},{1,0},{2,3},{3,2},{4,5},{5,4},{6,7},{7,6},{8,9},{9,8},{10,11... | collective-permute-start | bytes 2752520 | tf_op jit(solution)/shard_map/ppermute | solution.py:113
  491.6 306.6 %reduce-scatter.17.cloned.1.call-start = ((), (), s32[]{:S(2)}) async-start(), calls=%async_computation.13 | async-start | bytes 1114112 | tf_op jit(solution)/shard_map/reduce_scatter | solution.py:118
  514.7 287.4 %reduce-scatter.15.cloned.1.call-start = ((), (), s32[]{:S(2)}) async-start(), calls=%async_computation.12 | async-start | bytes 1114112 | tf_op jit(solution)/shard_map/reduce_scatter | solution.py:118
  530.2 369.1 %reduce-scatter.11.cloned.1.call-start = ((), (), s32[]{:S(2)}) async-start(), calls=%async_computation.10 | async-start | bytes 1114112 | tf_op jit(solution)/shard_map/reduce_scatter | solution.py:118
  544.8 414.8 %reduce-scatter.13.cloned.1.call-start = ((), (), s32[]{:S(2)}) async-start(), calls=%async_computation.11 | async-start | bytes 1114112 | tf_op jit(solution)/shard_map/reduce_scatter | solution.py:118
  552.5 538.2 %reduce-scatter.27.cloned.1.call-start = ((), (), s32[]{:S(2)}) async-start(), calls=%async_computation.18 | async-start | bytes 4456448 | tf_op jit(solution)/shard_map/reduce_scatter | solution.py:118
  561.5 623.2 %reduce-scatter.29.cloned.1.call-start = ((), (), s32[]{:S(2)}) async-start(), calls=%async_computation.19 | async-start | bytes 4456448 | tf_op jit(solution)/shard_map/reduce_scatter | solution.py:118
  565.6 36.6 %collective-permute-start.12 = (bf16[1500,512]{1,0:T(8,128)(2,1)S(1)}, bf16[1500,512]{1,0:T(8,128)(2,1)S(1)}, u32[]{:S(2)}, u32[]{:S(2)}) collective-permute-start(bf16[1500,512]{1,0:T(8,128)(2,1)S(1)} %fusion.36), channel_id=1, source_target_pairs={{0,1},{1,0},{2,3},{3,2},{4,5},{5,4},{6,7},{7,6},{8,9},{9,8},{10,11... | collective-permute-start | bytes 4608008 | tf_op jit(solution)/shard_map/ppermute | solution.py:315
  573.4 126.3 %collective-permute-start.8 = (bf16[448,1024]{1,0:T(8,128)(2,1)}, bf16[448,1024]{1,0:T(8,128)(2,1)}, u32[]{:S(2)}, u32[]{:S(2)}) collective-permute-start(bf16[448,1024]{1,0:T(8,128)(2,1)} %add_convert_fusion.1), channel_id=1, source_target_pairs={{0,1},{1,0},{2,3},{3,2},{4,5},{5,4},{6,7},{7,6},{8,9},{9,8},{10,11... | collective-permute-start | bytes 2752520 | tf_op jit(solution)/shard_map/ppermute | solution.py:113
  621.4 36.2 %collective-permute-start.13 = (bf16[1500,512]{1,0:T(8,128)(2,1)}, bf16[1500,512]{1,0:T(8,128)(2,1)}, u32[]{:S(2)}, u32[]{:S(2)}) collective-permute-start(bf16[1500,512]{1,0:T(8,128)(2,1)} %fusion.37), channel_id=1, source_target_pairs={{0,1},{1,0},{2,3},{3,2},{4,5},{5,4},{6,7},{7,6},{8,9},{9,8},{10,11... | collective-permute-start | bytes 4608008 | tf_op jit(solution)/shard_map/ppermute | solution.py:315
  634.6 66.3 %collective-permute-start.11 = (bf16[448,1024]{1,0:T(8,128)(2,1)}, bf16[448,1024]{1,0:T(8,128)(2,1)}, u32[]{:S(2)}, u32[]{:S(2)}) collective-permute-start(bf16[448,1024]{1,0:T(8,128)(2,1)} %add_convert_fusion), channel_id=1, source_target_pairs={{0,1},{1,0},{2,3},{3,2},{4,5},{5,4},{6,7},{7,6},{8,9},{9,8},{10,11... | collective-permute-start | bytes 2752520 | tf_op jit(solution)/shard_map/ppermute | solution.py:113
  661.7 17.2 %collective-permute-start.42 = (bf16[1,32,1024]{2,1,0:T(8,128)(2,1)}, bf16[1,32,1024]{2,1,0:T(8,128)(2,1)S(1)}, u32[]{:S(2)}, u32[]{:S(2)}) collective-permute-start(bf16[1,32,1024]{2,1,0:T(8,128)(2,1)} %bitcast.442), channel_id=1, source_target_pairs={{0,2},{2,0},{4,6},{6,4},{8,10},{10,8},{12,14},{14,12},{16,18},{18,... | collective-permute-start | bytes 196616 | tf_op jit(solution)/shard_map/ppermute | solution.py:23
  691.6 97.1 %collective-permute-start.44 = (bf16[4,32,1024]{2,1,0:T(8,128)(2,1)}, bf16[4,32,1024]{2,1,0:T(8,128)(2,1)}, u32[]{:S(2)}, u32[]{:S(2)}) collective-permute-start(bf16[4,32,1024]{2,1,0:T(8,128)(2,1)} %pad_maximum_fusion.45), channel_id=1, source_target_pairs={{0,8},{2,10},{4,12},{6,14},{8,0},{10,2},{12,4},{14,6},{16,24},{18,... | collective-permute-start | bytes 786440 | tf_op jit(solution)/shard_map/ppermute | solution.py:23
  694.4 96.2 %collective-permute-start.40 = (bf16[4,64,512]{2,1,0:T(8,128)(2,1)}, bf16[4,64,512]{2,1,0:T(8,128)(2,1)}, u32[]{:S(2)}, u32[]{:S(2)}) collective-permute-start(bf16[4,64,512]{2,1,0:T(8,128)(2,1)} %pad_maximum_fusion.44), channel_id=1, source_target_pairs={{0,8},{2,10},{4,12},{6,14},{8,0},{10,2},{12,4},{14,6},{16,24},{18,... | collective-permute-start | bytes 786440 | tf_op jit(solution)/shard_map/ppermute | solution.py:23
  697.2 98.1 %collective-permute-start.36 = (bf16[4,64,512]{2,1,0:T(8,128)(2,1)}, bf16[4,64,512]{2,1,0:T(8,128)(2,1)}, u32[]{:S(2)}, u32[]{:S(2)}) collective-permute-start(bf16[4,64,512]{2,1,0:T(8,128)(2,1)} %pad_maximum_fusion.43), channel_id=1, source_target_pairs={{0,8},{2,10},{4,12},{6,14},{8,0},{10,2},{12,4},{14,6},{16,24},{18,... | collective-permute-start | bytes 786440 | tf_op jit(solution)/shard_map/ppermute | solution.py:23
  699.8 97.5 %collective-permute-start.32 = (bf16[4,64,512]{2,1,0:T(8,128)(2,1)}, bf16[4,64,512]{2,1,0:T(8,128)(2,1)}, u32[]{:S(2)}, u32[]{:S(2)}) collective-permute-start(bf16[4,64,512]{2,1,0:T(8,128)(2,1)} %pad_maximum_fusion.42), channel_id=1, source_target_pairs={{0,8},{2,10},{4,12},{6,14},{8,0},{10,2},{12,4},{14,6},{16,24},{18,... | collective-permute-start | bytes 786440 | tf_op jit(solution)/shard_map/ppermute | solution.py:23
  790.6 172.7 %collective-permute-start.45 = (bf16[8,32,1024]{2,1,0:T(8,128)(2,1)}, bf16[8,32,1024]{2,1,0:T(8,128)(2,1)}, u32[]{:S(2)}, u32[]{:S(2)}) collective-permute-start(bf16[8,32,1024]{2,1,0:T(8,128)(2,1)} %pad_maximum_fusion.35), channel_id=1, source_target_pairs={{0,16},{2,18},{4,20},{6,22},{8,24},{10,26},{12,28},{14,30},{16,0},... | collective-permute-start | bytes 1572872 | tf_op jit(solution)/shard_map/ppermute | solution.py:23
  792.5 172.8 %collective-permute-start.41 = (bf16[8,64,512]{2,1,0:T(8,128)(2,1)}, bf16[8,64,512]{2,1,0:T(8,128)(2,1)}, u32[]{:S(2)}, u32[]{:S(2)}) collective-permute-start(bf16[8,64,512]{2,1,0:T(8,128)(2,1)} %pad_maximum_fusion.34), channel_id=1, source_target_pairs={{0,16},{2,18},{4,20},{6,22},{8,24},{10,26},{12,28},{14,30},{16,0},... | collective-permute-start | bytes 1572872 | tf_op jit(solution)/shard_map/ppermute | solution.py:23
  797.2 170.6 %collective-permute-start.37 = (bf16[8,64,512]{2,1,0:T(8,128)(2,1)}, bf16[8,64,512]{2,1,0:T(8,128)(2,1)}, u32[]{:S(2)}, u32[]{:S(2)}) collective-permute-start(bf16[8,64,512]{2,1,0:T(8,128)(2,1)} %pad_maximum_fusion.33), channel_id=1, source_target_pairs={{0,16},{2,18},{4,20},{6,22},{8,24},{10,26},{12,28},{14,30},{16,0},... | collective-permute-start | bytes 1572872 | tf_op jit(solution)/shard_map/ppermute | solution.py:23
  799.2 170.7 %collective-permute-start.33 = (bf16[8,64,512]{2,1,0:T(8,128)(2,1)}, bf16[8,64,512]{2,1,0:T(8,128)(2,1)}, u32[]{:S(2)}, u32[]{:S(2)}) collective-permute-start(bf16[8,64,512]{2,1,0:T(8,128)(2,1)} %pad_maximum_fusion.32), channel_id=1, source_target_pairs={{0,16},{2,18},{4,20},{6,22},{8,24},{10,26},{12,28},{14,30},{16,0},... | collective-permute-start | bytes 1572872 | tf_op jit(solution)/shard_map/ppermute | solution.py:23
  802.1 97.2 %collective-permute-start.22 = (bf16[1,64,512]{2,1,0:T(8,128)(2,1)}, bf16[1,64,512]{2,1,0:T(8,128)(2,1)S(1)}, u32[]{:S(2)}, u32[]{:S(2)}) collective-permute-start(bf16[1,64,512]{2,1,0:T(8,128)(2,1)} %bitcast.439), channel_id=1, source_target_pairs={{0,2},{2,0},{4,6},{6,4},{8,10},{10,8},{12,14},{14,12},{16,18},{18,... | collective-permute-start | bytes 196616 | tf_op jit(solution)/shard_map/ppermute | solution.py:23
  899.3 60.3 %collective-permute-start.14 = (bf16[1,64,512]{2,1,0:T(8,128)(2,1)}, bf16[1,64,512]{2,1,0:T(8,128)(2,1)}, u32[]{:S(2)}, u32[]{:S(2)}) collective-permute-start(bf16[1,64,512]{2,1,0:T(8,128)(2,1)} %bitcast.440), channel_id=1, source_target_pairs={{0,2},{2,0},{4,6},{6,4},{8,10},{10,8},{12,14},{14,12},{16,18},{18,... | collective-permute-start | bytes 196616 | tf_op jit(solution)/shard_map/ppermute | solution.py:23
  977.9 19.1 %collective-permute-start.28 = (bf16[4,32,1024]{2,1,0:T(8,128)(2,1)S(1)}, bf16[4,32,1024]{2,1,0:T(8,128)(2,1)S(1)}, u32[]{:S(2)}, u32[]{:S(2)}) collective-permute-start(bf16[4,32,1024]{2,1,0:T(8,128)(2,1)S(1)} %pad_maximum_fusion.41), channel_id=1, source_target_pairs={{0,8},{2,10},{4,12},{6,14},{8,0},{10,2},{12,4},{14,6},{16,24},{18,... | collective-permute-start | bytes 786440 | tf_op jit(solution)/shard_map/ppermute | solution.py:23
  979.4 17.5 %collective-permute-start.24 = (bf16[4,64,512]{2,1,0:T(8,128)(2,1)S(1)}, bf16[4,64,512]{2,1,0:T(8,128)(2,1)S(1)}, u32[]{:S(2)}, u32[]{:S(2)}) collective-permute-start(bf16[4,64,512]{2,1,0:T(8,128)(2,1)S(1)} %pad_maximum_fusion.40), channel_id=1, source_target_pairs={{0,8},{2,10},{4,12},{6,14},{8,0},{10,2},{12,4},{14,6},{16,24},{18,... | collective-permute-start | bytes 786440 | tf_op jit(solution)/shard_map/ppermute | solution.py:23
  980.2 39.7 %collective-permute-start.16 = (bf16[4,64,512]{2,1,0:T(8,128)(2,1)S(1)}, bf16[4,64,512]{2,1,0:T(8,128)(2,1)S(1)}, u32[]{:S(2)}, u32[]{:S(2)}) collective-permute-start(bf16[4,64,512]{2,1,0:T(8,128)(2,1)S(1)} %pad_maximum_fusion.38), channel_id=1, source_target_pairs={{0,8},{2,10},{4,12},{6,14},{8,0},{10,2},{12,4},{14,6},{16,24},{18,... | collective-permute-start | bytes 786440 | tf_op jit(solution)/shard_map/ppermute | solution.py:23
  981.6 46.8 %collective-permute-start.20 = (bf16[4,64,512]{2,1,0:T(8,128)(2,1)S(1)}, bf16[4,64,512]{2,1,0:T(8,128)(2,1)S(1)}, u32[]{:S(2)}, u32[]{:S(2)}) collective-permute-start(bf16[4,64,512]{2,1,0:T(8,128)(2,1)S(1)} %pad_maximum_fusion.39), channel_id=1, source_target_pairs={{0,8},{2,10},{4,12},{6,14},{8,0},{10,2},{12,4},{14,6},{16,24},{18,... | collective-permute-start | bytes 786440 | tf_op jit(solution)/shard_map/ppermute | solution.py:23
  996.9 93.8 %collective-permute-start.25 = (bf16[8,64,512]{2,1,0:T(8,128)(2,1)S(1)}, bf16[8,64,512]{2,1,0:T(8,128)(2,1)S(1)}, u32[]{:S(2)}, u32[]{:S(2)}) collective-permute-start(bf16[8,64,512]{2,1,0:T(8,128)(2,1)S(1)} %pad_maximum_fusion.30), channel_id=1, source_target_pairs={{0,16},{2,18},{4,20},{6,22},{8,24},{10,26},{12,28},{14,30},{16,0},... | collective-permute-start | bytes 1572872 | tf_op jit(solution)/shard_map/ppermute | solution.py:23
  997.9 96.5 %collective-permute-start.29 = (bf16[8,32,1024]{2,1,0:T(8,128)(2,1)}, bf16[8,32,1024]{2,1,0:T(8,128)(2,1)}, u32[]{:S(2)}, u32[]{:S(2)}) collective-permute-start(bf16[8,32,1024]{2,1,0:T(8,128)(2,1)} %pad_maximum_fusion.31), channel_id=1, source_target_pairs={{0,16},{2,18},{4,20},{6,22},{8,24},{10,26},{12,28},{14,30},{16,0},... | collective-permute-start | bytes 1572872 | tf_op jit(solution)/shard_map/ppermute | solution.py:23
  1021.5 167.4 %collective-permute-start.17 = (bf16[8,64,512]{2,1,0:T(8,128)(2,1)}, bf16[8,64,512]{2,1,0:T(8,128)(2,1)}, u32[]{:S(2)}, u32[]{:S(2)}) collective-permute-start(bf16[8,64,512]{2,1,0:T(8,128)(2,1)} %pad_maximum_fusion.28), channel_id=1, source_target_pairs={{0,16},{2,18},{4,20},{6,22},{8,24},{10,26},{12,28},{14,30},{16,0},... | collective-permute-start | bytes 1572872 | tf_op jit(solution)/shard_map/ppermute | solution.py:23
  1030.0 160.0 %collective-permute-start.21 = (bf16[8,64,512]{2,1,0:T(8,128)(2,1)}, bf16[8,64,512]{2,1,0:T(8,128)(2,1)}, u32[]{:S(2)}, u32[]{:S(2)}) collective-permute-start(bf16[8,64,512]{2,1,0:T(8,128)(2,1)} %pad_maximum_fusion.29), channel_id=1, source_target_pairs={{0,16},{2,18},{4,20},{6,22},{8,24},{10,26},{12,28},{14,30},{16,0},... | collective-permute-start | bytes 1572872 | tf_op jit(solution)/shard_map/ppermute | solution.py:23
  1093.4 91.3 %collective-permute-start.47 = (bf16[2,64,2048]{2,1,0:T(8,128)(2,1)}, bf16[2,64,2048]{2,1,0:T(8,128)(2,1)}, u32[]{:S(2)}, u32[]{:S(2)}) collective-permute-start(bf16[2,64,2048]{2,1,0:T(8,128)(2,1)} %pad_maximum_fusion.36), channel_id=1, source_target_pairs={{0,4},{2,6},{4,0},{6,2},{8,12},{10,14},{12,8},{14,10},{16,20},{18,... | collective-permute-start | bytes 1572872 | tf_op jit(solution)/shard_map/ppermute | solution.py:23
  1186.2 25.6 %collective-permute-start.48 = (bf16[4,64,2048]{2,1,0:T(8,128)(2,1)S(1)}, bf16[4,64,2048]{2,1,0:T(8,128)(2,1)S(1)}, u32[]{:S(2)}, u32[]{:S(2)}) collective-permute-start(bf16[4,64,2048]{2,1,0:T(8,128)(2,1)S(1)} %pad_maximum_fusion.23), channel_id=1, source_target_pairs={{0,8},{2,10},{4,12},{6,14},{8,0},{10,2},{12,4},{14,6},{16,24},{18,... | collective-permute-start | bytes 3145736 | tf_op jit(solution)/shard_map/ppermute | solution.py:23
  1212.1 138.3 %collective-permute-start.49 = (bf16[8,64,2048]{2,1,0:T(8,128)(2,1)S(1)}, bf16[8,64,2048]{2,1,0:T(8,128)(2,1)S(1)}, u32[]{:S(2)}, u32[]{:S(2)}) collective-permute-start(bf16[8,64,2048]{2,1,0:T(8,128)(2,1)S(1)} %pad_maximum_fusion.8), channel_id=1, source_target_pairs={{0,16},{2,18},{4,20},{6,22},{8,24},{10,26},{12,28},{14,30},{16,0},... | collective-permute-start | bytes 6291464 | tf_op jit(solution)/shard_map/ppermute | solution.py:23
  1213.6 67.1 %collective-permute-start.52 = (bf16[4,128,1024]{2,1,0:T(8,128)(2,1)S(1)}, bf16[4,128,1024]{2,1,0:T(8,128)(2,1)S(1)}, u32[]{:S(2)}, u32[]{:S(2)}) collective-permute-start(bf16[4,128,1024]{2,1,0:T(8,128)(2,1)S(1)} %pad_maximum_fusion.24), channel_id=1, source_target_pairs={{0,8},{2,10},{4,12},{6,14},{8,0},{10,2},{12,4},{14,6},{16,24},{18,... | collective-permute-start | bytes 3145736 | tf_op jit(solution)/shard_map/ppermute | solution.py:23
  1281.0 114.1 %collective-permute-start.53 = (bf16[8,128,1024]{2,1,0:T(8,128)(2,1)S(1)}, bf16[8,128,1024]{2,1,0:T(8,128)(2,1)S(1)}, u32[]{:S(2)}, u32[]{:S(2)}) collective-permute-start(bf16[8,128,1024]{2,1,0:T(8,128)(2,1)S(1)} %pad_maximum_fusion.9), channel_id=1, source_target_pairs={{0,16},{2,18},{4,20},{6,22},{8,24},{10,26},{12,28},{14,30},{16,0},... | collective-permute-start | bytes 6291464 | tf_op jit(solution)/shard_map/ppermute | solution.py:23
  (212 other events, 1898.1 us)
Sparse Core Ops, SparseCore 0:
  412.8 58.0 reduce-scatter.24
  474.5 56.6 reduce-scatter.22
  534.8 56.5 reduce-scatter.20
  594.9 56.6 reduce-scatter.18
  655.0 59.6 reduce-scatter.16
  718.2 56.6 reduce-scatter.14
  778.5 120.7 reduce-scatter.10
  902.9 56.6 reduce-scatter.12
  964.0 126.6 reduce-scatter.26
  1095.0 89.6 reduce-scatter.28
